TPU v7x, 32 devices: a whole 2x2x4 slice. The times are simulated.
32 devices in a mesh: dp: 4 (over x, core), seq: 4 (over z), chan: 2 (over y).
Axes of the slice: x: 2, y: 2, z: 4, core: 2. Of those that a mesh axis runs over, the one named last changes fastest.
Arguments:
- inputs: bfloat16 [4, 8, 256, 2048], P('dp', 'seq', None, 'chan'), may hold values from -6 to 6
- cotangent: bfloat16 [4, 8, 256, 2048], P('dp', 'seq', None, 'chan'), may hold values from -6 to 6
- rows_in: bfloat16 [256, 256], replicated, may hold values from -0.375 to 0.375
- cols_mix: bfloat16 [8, 8], replicated, may hold values from -2 to 2
- blocks_gate: bfloat16 [4, 512, 512], P('chan'), may hold values from -0.25 to 0.25
- blocks_up: bfloat16 [4, 512, 512], P('chan'), may hold values from -0.25 to 0.25
- mix_gate: bfloat16 [4, 4, 512], replicated, may hold values from -3 to 3
- mix_up: bfloat16 [4, 4, 512], replicated, may hold values from -3 to 3
Outputs:
- input_grad: bfloat16 [4, 8, 256, 2048], P('dp', 'seq', None, 'chan')
- rows_grad: float32 [256, 256], replicated
- cols_grad: float32 [8, 8], replicated
- blocks_gate_grad: float32 [4, 512, 512], P('chan')
- blocks_up_grad: float32 [4, 512, 512], P('chan')
- mix_gate_grad: float32 [4, 4, 512], P(None, 'chan')
- mix_up_grad: float32 [4, 4, 512], P(None, 'chan')
All inputs are finite; a program needn't handle non-finite values.
Results may differ from a plain program's by a relative error of at most 0.011.
Values may be sent and summed in bfloat16 or wider, within the bound.
No kernel may reach another device: no remote copies, remote signals or barrier semaphores. Data moves between devices by JAX's collectives and lax.ppermute only.
A program may use at most 128 MiB of HBM per device.

v0:
```python
import math
import jax
import jax.numpy as jnp
from jax import lax
from jax.sharding import PartitionSpec as P


def column_keep(segment, cols_mix):
    mixed = jnp.einsum(
        "er,brcd->becd", cols_mix, segment, preferred_element_type=jnp.float32
    ).astype(jnp.bfloat16)
    return (segment, mixed)


def body(inputs, cotangent, rows_in, cols_mix, blocks_gate, blocks_up, mix_gate, mix_up):
    batch_dev, rows_dev, cols_all, width_dev = inputs.shape
    block_size = blocks_gate.shape[1]
    local_blocks = blocks_gate.shape[0]
    chan_index = lax.axis_index("chan")
    split_shape = (batch_dev, rows_dev, cols_all, local_blocks, block_size)
    first = jnp.einsum("ec,brcd->bred", rows_in, inputs, preferred_element_type=jnp.float32).astype(
        jnp.bfloat16
    )
    first_cols, second_cols = column_keep(
        lax.all_to_all(first, "seq", split_axis=2, concat_axis=1, tiled=True), cols_mix
    )
    second_rows = lax.all_to_all(second_cols, "seq", split_axis=1, concat_axis=2, tiled=True)
    hidden = (inputs.astype(jnp.float32) + second_rows.astype(jnp.float32)).astype(jnp.bfloat16)
    hidden_blocks = hidden.reshape(split_shape)
    gate_rows_own = lax.dynamic_slice_in_dim(
        mix_gate, chan_index * local_blocks, local_blocks, 0
    ).astype(jnp.float32)
    up_rows_own = lax.dynamic_slice_in_dim(
        mix_up, chan_index * local_blocks, local_blocks, 0
    ).astype(jnp.float32)
    gate_mid = jnp.einsum(
        "brckj,kjl->brckl", hidden_blocks, blocks_gate, preferred_element_type=jnp.float32
    ).astype(jnp.bfloat16)
    up_mid = jnp.einsum(
        "brckj,kjl->brckl", hidden_blocks, blocks_up, preferred_element_type=jnp.float32
    ).astype(jnp.bfloat16)
    gate_add = jnp.einsum(
        "mkj,brckj->brcmj",
        gate_rows_own,
        lax.all_gather(gate_mid, "chan", axis=3, tiled=True).astype(jnp.float32),
    )
    up_add = jnp.einsum(
        "mkj,brckj->brcmj",
        up_rows_own,
        lax.all_gather(up_mid, "chan", axis=3, tiled=True).astype(jnp.float32),
    )
    upstream = cotangent.astype(jnp.float32).reshape(split_shape)
    sigma = jax.nn.sigmoid(gate_add)
    up_grad = (upstream * gate_add * sigma).astype(jnp.bfloat16)
    gate_grad = (upstream * up_add * sigma * (1.0 + gate_add * (1.0 - sigma))).astype(jnp.bfloat16)
    gate_all, up_all = (
        lax.all_gather(gate_grad, "chan", axis=3, tiled=True),
        lax.all_gather(up_grad, "chan", axis=3, tiled=True),
    )
    gate_cols_own = lax.dynamic_slice_in_dim(
        mix_gate, chan_index * local_blocks, local_blocks, 1
    ).astype(jnp.float32)
    up_cols_own = lax.dynamic_slice_in_dim(
        mix_up, chan_index * local_blocks, local_blocks, 1
    ).astype(jnp.float32)
    mix_gate_sum = jnp.einsum(
        "brcmj,brckj->mkj", gate_all, gate_mid, preferred_element_type=jnp.float32
    )
    mix_up_sum = jnp.einsum("brcmj,brckj->mkj", up_all, up_mid, preferred_element_type=jnp.float32)
    gate_back = jnp.einsum("mkj,brcmj->brckj", gate_cols_own, gate_all.astype(jnp.float32)).astype(
        jnp.bfloat16
    )
    up_back = jnp.einsum("mkj,brcmj->brckj", up_cols_own, up_all.astype(jnp.float32)).astype(
        jnp.bfloat16
    )
    blocks_gate_sum = jnp.einsum(
        "brckj,brckl->kjl", hidden_blocks, gate_back, preferred_element_type=jnp.float32
    )
    blocks_up_sum = jnp.einsum(
        "brckj,brckl->kjl", hidden_blocks, up_back, preferred_element_type=jnp.float32
    )
    hidden_grad = (
        upstream
        + jnp.einsum("brckl,kjl->brckj", gate_back, blocks_gate, preferred_element_type=jnp.float32)
        + jnp.einsum("brckl,kjl->brckj", up_back, blocks_up, preferred_element_type=jnp.float32)
    )
    hidden_grad = hidden_grad.reshape(inputs.shape).astype(jnp.bfloat16)
    segment = lax.all_to_all(hidden_grad, "seq", split_axis=2, concat_axis=1, tiled=True)
    mixed = jnp.einsum(
        "er,becd->brcd", cols_mix, segment, preferred_element_type=jnp.float32
    ).astype(jnp.bfloat16)
    cols_sum = jnp.einsum("becd,brcd->er", segment, first_cols, preferred_element_type=jnp.float32)
    first_grad = lax.all_to_all(mixed, "seq", split_axis=1, concat_axis=2, tiled=True)
    rows_sum = jnp.einsum("bred,brcd->ec", first_grad, inputs, preferred_element_type=jnp.float32)
    input_grad = (
        hidden_grad.astype(jnp.float32)
        + jnp.einsum("ec,bred->brcd", rows_in, first_grad, preferred_element_type=jnp.float32)
    ).astype(jnp.bfloat16)
    rows_total, cols_total = lax.psum((rows_sum, cols_sum), ("dp", "seq", "chan"))
    gate_blocks_total, up_blocks_total, gate_mix_total, up_mix_total = lax.psum(
        (blocks_gate_sum, blocks_up_sum, mix_gate_sum, mix_up_sum), ("dp", "seq")
    )
    count_dp = lax.axis_size("dp")
    count_seq = lax.axis_size("seq")
    count_chan = lax.axis_size("chan")
    batch_all = batch_dev * count_dp
    rows_all = rows_dev * count_seq
    width_all = width_dev * count_chan
    rows_scale = 1.0 / math.sqrt(batch_all * rows_all * width_all)
    cols_scale = 1.0 / math.sqrt(batch_all * cols_all * width_all)
    block_scale = 1.0 / math.sqrt(batch_all * rows_all * cols_all)
    return (
        input_grad,
        rows_total * rows_scale,
        cols_total * cols_scale,
        gate_blocks_total * block_scale,
        up_blocks_total * block_scale,
        gate_mix_total * block_scale,
        up_mix_total * block_scale,
    )


def solution(mesh):
    in_specs = (
        P("dp", "seq", None, "chan"),
        P("dp", "seq", None, "chan"),
        P(),
        P(),
        P("chan", None, None),
        P("chan", None, None),
        P(),
        P(),
    )
    out_specs = (
        P("dp", "seq", None, "chan"),
        P(),
        P(),
        P("chan", None, None),
        P("chan", None, None),
        P(None, "chan", None),
        P(None, "chan", None),
    )
    return jax.shard_map(body, mesh=mesh, in_specs=in_specs, out_specs=out_specs, check_vma=False)
```

profile of v0, /device:TPU:0, one launch (start us, length us, event | category | flops | bytes accessed | tf_op | source)
XLA Modules:
  0.0 618.1 jit_solution(10451862501799467449)
XLA Ops:
  10.1 31.8 %all_to_all.54 = bf16[1,2,256,1024]{3,1,0,2:T(2,128)(2,1)S(1)} all-to-all(bf16[1,2,256,1024]{3,1,0,2:T(2,128)(2,1)S(1)} %copy.163), channel_id=1, replica_groups=mesh['dp'=4,'seq'=4,'chan'=2] {'seq'}, dimensions={2} | all-to-all | bytes 2097152 | tf_op jit(solution)/shard_map/all_to_all | solution.py:25
  44.9 27.8 %all_to_all.55 = bf16[1,8,64,1024]{3,2,0,1:T(8,128)(2,1)S(1)} all-to-all(bf16[1,8,64,1024]{3,2,0,1:T(8,128)(2,1)S(1)} %copy.166), channel_id=1, replica_groups=mesh['dp'=4,'seq'=4,'chan'=2] {'seq'}, dimensions={1} | all-to-all | bytes 2097152 | tf_op jit(solution)/shard_map/all_to_all | solution.py:27
  88.8 26.0 %all-gather.5.cloned.1.call-done = bf16[1,2,256,4,512]{4,2,1,0,3:T(8,128)(2,1)} async-done(((bf16[1,2,256,2,512]{4,2,1,0,3:T(8,128)(2,1)}), bf16[1,2,256,4,512]{4,2,1,0,3:T(8,128)(2,1)}) %all-gather.5.cloned.1.call-update) | async-done | bytes 2097168 | tf_op jit(solution)/shard_map/all_gather | solution.py:50
  114.8 4.5 copy.170
  119.3 4.2 fusion.14
  123.5 4.2 copy.172
  127.7 22.4 %all-gather.7.cloned.1.call-done = bf16[1,2,256,4,512]{4,2,1,0,3:T(8,128)(2,1)} async-done(((bf16[1,2,256,2,512]{4,2,1,0,3:T(8,128)(2,1)}), bf16[1,2,256,4,512]{4,2,1,0,3:T(8,128)(2,1)}) %all-gather.7.cloned.1.call-update) | async-done | bytes 2097168 | tf_op jit(solution)/shard_map/all_gather | solution.py:45
  150.1 4.5 copy.176
  154.6 4.1 fusion.12
  158.7 4.1 copy.178
  162.9 5.0 fusion.10
  173.4 28.8 %all-gather.11.cloned.1.call-done = bf16[1,2,256,4,512]{4,2,1,0,3:T(8,128)(2,1)} async-done(((bf16[1,2,256,2,512]{4,2,1,0,3:T(8,128)(2,1)}), bf16[1,2,256,4,512]{4,2,1,0,3:T(8,128)(2,1)}) %all-gather.11.cloned.1.call-update) | async-done | bytes 2097168 | tf_op jit(solution)/shard_map/all_gather | solution.py:58
  202.2 4.5 copy.186
  206.7 3.9 fusion.30
  213.1 24.3 %all-gather.9.cloned.1.call-done = bf16[1,2,256,4,512]{4,2,1,0,3:T(8,128)(2,1)} async-done(((bf16[1,2,256,2,512]{4,2,1,0,3:T(8,128)(2,1)}), bf16[1,2,256,4,512]{4,2,1,0,3:T(8,128)(2,1)}) %all-gather.9.cloned.1.call-update) | async-done | bytes 2097168 | tf_op jit(solution)/shard_map/all_gather | solution.py:57
  237.3 4.5 copy.180
  254.9 4.6 all-to-all-start.2
  269.1 23.6 %all-to-all-done.2 = bf16[1,2,256,1024]{3,1,0,2:T(2,128)(2,1)} async-done(((bf16[1,2,256,1024]{3,1,0,2:T(2,128)(2,1)}), bf16[1,2,256,1024]{3,1,0,2:T(2,128)(2,1)}, u32[]{:S(2)}, u32[]{:S(2)}) %all-to-all-start.2) | async-done | bytes 1048608 | tf_op jit(solution)/shard_map/all_to_all | solution.py:88
  297.8 4.3 all-to-all-start.3
  302.1 5.5 fusion.39
  311.1 120.2 %all-reduce = (f32[4,2,512]{0,1,2:T(2,128)}, f32[4,2,512]{0,1,2:T(2,128)}) all-reduce(f32[4,2,512]{0,1,2:T(2,128)} %fusion.39, f32[4,2,512]{0,1,2:T(2,128)} %fusion.42), channel_id=1, replica_groups=mesh['dp'=4,'seq'=4,'chan'=2] {'dp','seq'}, use_global_device_ids=true, to_apply=%region_4.0 | all-reduce | flops 8192 | bytes 65536 | tf_op jit(solution)/shard_map/psum | solution.py:100
  438.5 36.9 %psum.43 = f32[8,8]{1,0:T(8,128)S(1)} all-reduce(f32[8,8]{1,0:T(8,128)S(1)} %convolution_bitcast_fusion.3), channel_id=1, replica_groups=mesh['dp'=4,'seq'=4,'chan'=2] {'dp','seq','chan'}, use_global_device_ids=true, to_apply=%region_1.0 | all-reduce | flops 64 | bytes 512 | tf_op jit(solution)/shard_map/psum | solution.py:99
  475.9 4.7 broadcast_multiply_fusion
  487.2 122.4 %all-reduce.5.cloned.1.call-done = f32[256,256]{1,0:T(8,128)} async-done(((f32[256,256]{1,0:T(8,128)}), f32[256,256]{1,0:T(8,128)}) %all-reduce.5.cloned.1.call-update) | async-done | bytes 262160 | tf_op jit(solution)/shard_map/psum | solution.py:99
  (108 shorter events, 76.8 us)
Async XLA Ops:
  7.2 75.4 %copy-start = (bf16[2,512,512]{2,1,0:T(8,128)(2,1)S(1)}, bf16[2,512,512]{2,1,0:T(8,128)(2,1)}, u32[]{:S(2)}) copy-start(bf16[2,512,512]{2,1,0:T(8,128)(2,1)} %param.12) | copy-start | bytes 3145732
  7.2 107.7 %all-gather.5.cloned.1.call-start = ((), (), s32[]{:S(2)}) async-start(), calls=%async_computation.4 | async-start | bytes 3145728 | tf_op jit(solution)/shard_map/all_gather | solution.py:50
  42.3 1.6 copy-start.19
  75.5 5.1 copy-start.12
  82.4 2.1 copy-start.17
  82.5 3.0 copy-start.18
  82.5 67.6 %all-gather.7.cloned.1.call-start = ((), (), s32[]{:S(2)}) async-start(), calls=%async_computation.5 | async-start | bytes 3145728 | tf_op jit(solution)/shard_map/all_gather | solution.py:45
  84.3 117.9 %all-gather.11.cloned.1.call-start = ((), (), s32[]{:S(2)}) async-start(), calls=%async_computation.7 | async-start | bytes 3145728 | tf_op jit(solution)/shard_map/all_gather | solution.py:58
  168.9 68.4 %all-gather.9.cloned.1.call-start = ((), (), s32[]{:S(2)}) async-start(), calls=%async_computation.6 | async-start | bytes 3145728 | tf_op jit(solution)/shard_map/all_gather | solution.py:57
  213.0 38.4 %copy-start.6 = (bf16[2,256,2,512]{3,1,0,2:T(8,128)(2,1)}, bf16[2,256,2,512]{3,1,0,2:T(8,128)(2,1)S(1)}, u32[]{:S(2)}) copy-start(bf16[2,256,2,512]{3,1,0,2:T(8,128)(2,1)S(1)} %copy.188) | copy-start | bytes 3145732
  249.3 2.1 copy-start.11
  249.3 2.2 copy-start.13
  252.8 6.8 %copy-start.7 = (bf16[2,256,2,512]{3,1,0,2:T(8,128)(2,1)S(1)}, bf16[2,256,2,512]{3,1,0,2:T(8,128)(2,1)}, u32[]{:S(2)}) copy-start(bf16[2,256,2,512]{3,1,0,2:T(8,128)(2,1)} %copy-done.6) | copy-start | bytes 3145732
  254.9 37.7 %all-to-all-start.2 = ((bf16[1,2,256,1024]{3,1,0,2:T(2,128)(2,1)}), bf16[1,2,256,1024]{3,1,0,2:T(2,128)(2,1)}, u32[]{:S(2)}, u32[]{:S(2)}) async-start(bf16[1,2,256,1024]{3,1,0,2:T(2,128)(2,1)} %copy.190), calls=%async_computation.2 | async-start | bytes 2097152 | tf_op jit(solution)/shard_map/all_to_all | solution.py:88
  259.5 216.4 %all-reduce.7.cloned.1.call-start = ((), (), s32[]{:S(2)}) async-start(), calls=%async_computation.9 | async-start | bytes 8388608 | tf_op jit(solution)/shard_map/psum | solution.py:100
  259.6 2.0 copy-start.10
  263.7 3.3 copy-start.4
  297.8 182.9 %all-to-all-start.3 = ((bf16[1,8,64,1024]{3,2,0,1:T(8,128)(2,1)}), bf16[1,8,64,1024]{3,2,0,1:T(8,128)(2,1)}, u32[]{:S(2)}, u32[]{:S(2)}) async-start(bf16[1,8,64,1024]{3,2,0,1:T(8,128)(2,1)} %copy.194), calls=%async_computation.3 | async-start | bytes 2097152 | tf_op jit(solution)/shard_map/all_to_all | solution.py:93
  302.1 5.5 copy-start.15
  302.1 307.5 %all-reduce.5.cloned.1.call-start = ((), (), s32[]{:S(2)}) async-start(), calls=%async_computation.8 | async-start | bytes 524288 | tf_op jit(solution)/shard_map/psum | solution.py:99
  302.1 5.5 copy-start.14
  311.1 126.6 %copy-start.3 = (bf16[8,64,1024]{2,0,1:T(8,128)(2,1)S(1)}, bf16[8,64,1024]{2,0,1:T(8,128)(2,1)}, u32[]{:S(2)}) copy-start(bf16[8,64,1024]{2,0,1:T(8,128)(2,1)} %copy-done.2) | copy-start | bytes 3145732
  480.7 2.7 copy-start.16
  483.4 127.9 %copy-start.1 = (bf16[2,512,512]{2,1,0:T(8,128)(2,1)S(1)}, bf16[2,512,512]{2,1,0:T(8,128)(2,1)}, u32[]{:S(2)}) copy-start(bf16[2,512,512]{2,1,0:T(8,128)(2,1)} %param.12) | copy-start | bytes 3145732
  (4 other events, 5.0 us)
Sparse Core Ops, SparseCore 0:
  82.6 32.2 all-gather.4
  117.0 33.1 all-gather.6
  169.0 33.1 all-gather.10
  204.2 33.1 all-gather.8
  264.4 161.0 all-reduce.6
  483.5 126.0 all-reduce.4
where the time goes:
time: 620 us; the launch traced here: 618 us
  waiting for transfers between devices  248 us (40%)
  blocking collectives  217 us (35%)
  local copies, waits for them, and re-layouts  72.1 us (12%)
  matrix products  41.5 us (7%)
  other arithmetic  16.3 us (3%)
  between operations  14.5 us (2%)
  starting transfers between devices  9.24 us (1%)
    psum x1, waiting for transfers between devices, body(): lax.psum((rows_sum, cols_sum), ('dp', 'seq', 'chan'))  122 us
    psum x1, blocking collectives, body(): lax.psum((blocks_gate_sum, blocks_up_sum, mix_gate_sum, mix_up_sum), ('dp...  120 us
    psum x1, blocking collectives, body(): lax.psum((rows_sum, cols_sum), ('dp', 'seq', 'chan'))  36.9 us
    all_to_all x1, blocking collectives, body(): lax.all_to_all(first, 'seq', split_axis=2, concat_axis=1, tiled=True)  31.8 us
    all_gather x1, waiting for transfers between devices, body(): lax.all_gather(up_grad, 'chan', axis=3, tiled=True)  28.8 us
    all_to_all x1, blocking collectives, body(): lax.all_to_all(second_cols, 'seq', split_axis=1, concat_axis=2, tiled=True)  27.8 us
    all_gather x1, waiting for transfers between devices, body(): lax.all_gather(up_mid, 'chan', axis=3, tiled=True).astype(jnp.float32)  26 us
    all_gather x1, waiting for transfers between devices, body(): lax.all_gather(gate_grad, 'chan', axis=3, tiled=True)  24.3 us
  transfers between devices with their start and end apart: 8, of which 6 were waited for; matrix products, arithmetic and copies ran while one was open for 12% of the time, Pallas kernels for 0%

commit v1 on v0

--- a/solution.py
+++ b/solution.py
@@ -98,7 +98,7 @@
     ).astype(jnp.bfloat16)
     rows_total, cols_total = lax.psum((rows_sum, cols_sum), ("dp", "seq", "chan"))
     gate_blocks_total, up_blocks_total, gate_mix_total, up_mix_total = lax.psum(
-        (blocks_gate_sum, blocks_up_sum, mix_gate_sum, mix_up_sum), ("dp", "seq")
+        lax.psum((blocks_gate_sum, blocks_up_sum, mix_gate_sum, mix_up_sum), "seq"), "dp"
     )
     count_dp = lax.axis_size("dp")
     count_seq = lax.axis_size("seq")

time: 620 us -> 685 us (1.10)
  blocking collectives: 217 us -> 278 us
  waiting for transfers between devices: 248 us -> 264 us
  starting transfers between devices: 9.24 us -> 0.69 us
    psum x1 -> x2, waiting for transfers between devices: 0.01 us -> 164 us  [the longest x1 85.6 us: body(): lax.psum(lax.psum((blocks_gate_sum, blocks_up_sum, mix_gate_sum, mix_up_s...]
    psum x1, waiting for transfers between devices: 122 us -> 0.09 us  [body(): lax.psum((rows_sum, cols_sum), ('dp', 'seq', 'chan'))]
    all_to_all x0 -> x2, blocking collectives: none -> 108 us  [the longest x1 58.1 us: body(): lax.all_to_all(hidden_grad, 'seq', split_axis=2, concat_axis=1, tiled=True)]
    psum x1 -> x2, blocking collectives: 120 us -> 69.9 us  [the longest x1 43.2 us: body(): lax.psum((blocks_gate_sum, blocks_up_sum, mix_gate_sum, mix_up_sum), 'seq')]
    all_to_all x2 -> x0, waiting for transfers between devices: 23.6 us -> none  [the longest x1 23.6 us: body(): lax.all_to_all(hidden_grad, 'seq', split_axis=2, concat_axis=1, tiled=True)]
    all_to_all x2 -> x0, starting transfers between devices: 8.85 us -> none  [the longest x1 4.6 us: body(): lax.all_to_all(hidden_grad, 'seq', split_axis=2, concat_axis=1, tiled=True)]
  transfers between devices with their start and end apart: 8 -> 7, of which waited for: 6 -> 7; matrix products, arithmetic and copies ran while one was open for 12% -> 10% of each run, Pallas kernels for 0% -> 0%
where the time goes in v1:
time: 685 us; the launch traced here: 684 us
  blocking collectives  278 us (41%)
  waiting for transfers between devices  264 us (39%)
  local copies, waits for them, and re-layouts  68.6 us (10%)
  matrix products  43.2 us (6%)
  other arithmetic  15.2 us (2%)
  between operations  14.5 us (2%)
    psum x1, waiting for transfers between devices, body(): lax.psum(lax.psum((blocks_gate_sum, blocks_up_sum, mix_gate_sum, mix_up_s...  85.6 us
    psum x1, waiting for transfers between devices, body(): lax.psum((blocks_gate_sum, blocks_up_sum, mix_gate_sum, mix_up_sum), 'seq')  78.7 us
    all_to_all x1, blocking collectives, body(): lax.all_to_all(hidden_grad, 'seq', split_axis=2, concat_axis=1, tiled=True)  58.1 us
    all_to_all x1, blocking collectives, body(): lax.all_to_all(mixed, 'seq', split_axis=1, concat_axis=2, tiled=True)  50.1 us
    psum x1, blocking collectives, body(): lax.psum((blocks_gate_sum, blocks_up_sum, mix_gate_sum, mix_up_sum), 'seq')  43.2 us
    psum x1, blocking collectives, body(): lax.psum((rows_sum, cols_sum), ('dp', 'seq', 'chan'))  39.9 us
    all_to_all x1, blocking collectives, body(): lax.all_to_all(first, 'seq', split_axis=2, concat_axis=1, tiled=True)  31.8 us
    all_gather x1, waiting for transfers between devices, body(): lax.all_gather(up_grad, 'chan', axis=3, tiled=True)  28.8 us
  transfers between devices with their start and end apart: 7, of which 7 were waited for; matrix products, arithmetic and copies ran while one was open for 10% of the time, Pallas kernels for 0%

profile of v1, /device:TPU:0, one launch (start us, length us, event | category | flops | bytes accessed | tf_op | source)
XLA Modules:
  0.0 683.6 jit_solution(17059473160936973338)
XLA Ops:
  10.1 31.8 %all_to_all.54 = bf16[1,2,256,1024]{3,1,0,2:T(2,128)(2,1)S(1)} all-to-all(bf16[1,2,256,1024]{3,1,0,2:T(2,128)(2,1)S(1)} %copy.163), channel_id=1, replica_groups=mesh['dp'=4,'seq'=4,'chan'=2] {'seq'}, dimensions={2} | all-to-all | bytes 2097152 | tf_op jit(solution)/shard_map/all_to_all | solution.py:25
  44.9 27.8 %all_to_all.55 = bf16[1,8,64,1024]{3,2,0,1:T(8,128)(2,1)S(1)} all-to-all(bf16[1,8,64,1024]{3,2,0,1:T(8,128)(2,1)S(1)} %copy.166), channel_id=1, replica_groups=mesh['dp'=4,'seq'=4,'chan'=2] {'seq'}, dimensions={1} | all-to-all | bytes 2097152 | tf_op jit(solution)/shard_map/all_to_all | solution.py:27
  86.7 26.0 %all-gather.5.cloned.1.call-done = bf16[1,2,256,4,512]{4,2,1,0,3:T(8,128)(2,1)} async-done(((bf16[1,2,256,2,512]{4,2,1,0,3:T(8,128)(2,1)}), bf16[1,2,256,4,512]{4,2,1,0,3:T(8,128)(2,1)}) %all-gather.5.cloned.1.call-update) | async-done | bytes 2097168 | tf_op jit(solution)/shard_map/all_gather | solution.py:50
  112.7 4.5 copy.170
  117.2 4.2 fusion.14
  121.4 4.3 copy.172
  125.7 22.3 %all-gather.7.cloned.1.call-done = bf16[1,2,256,4,512]{4,2,1,0,3:T(8,128)(2,1)} async-done(((bf16[1,2,256,2,512]{4,2,1,0,3:T(8,128)(2,1)}), bf16[1,2,256,4,512]{4,2,1,0,3:T(8,128)(2,1)}) %all-gather.7.cloned.1.call-update) | async-done | bytes 2097168 | tf_op jit(solution)/shard_map/all_gather | solution.py:45
  148.0 4.5 copy.176
  152.5 4.1 fusion.12
  156.6 4.1 copy.178
  160.8 5.0 fusion.10
  171.3 28.8 %all-gather.11.cloned.1.call-done = bf16[1,2,256,4,512]{4,2,1,0,3:T(8,128)(2,1)} async-done(((bf16[1,2,256,2,512]{4,2,1,0,3:T(8,128)(2,1)}), bf16[1,2,256,4,512]{4,2,1,0,3:T(8,128)(2,1)}) %all-gather.11.cloned.1.call-update) | async-done | bytes 2097168 | tf_op jit(solution)/shard_map/all_gather | solution.py:58
  200.1 4.5 copy.186
  213.1 22.2 %all-gather.9.cloned.1.call-done = bf16[1,2,256,4,512]{4,2,1,0,3:T(8,128)(2,1)} async-done(((bf16[1,2,256,2,512]{4,2,1,0,3:T(8,128)(2,1)}), bf16[1,2,256,4,512]{4,2,1,0,3:T(8,128)(2,1)}) %all-gather.9.cloned.1.call-update) | async-done | bytes 2097168 | tf_op jit(solution)/shard_map/all_gather | solution.py:57
  235.2 4.5 copy.180
  258.3 58.1 %all_to_all.56 = bf16[1,2,256,1024]{3,1,0,2:T(2,128)(2,1)S(1)} all-to-all(bf16[1,2,256,1024]{3,1,0,2:T(2,128)(2,1)S(1)} %copy.190), channel_id=1, replica_groups=mesh['dp'=4,'seq'=4,'chan'=2] {'seq'}, dimensions={2} | all-to-all | bytes 2097152 | tf_op jit(solution)/shard_map/all_to_all | solution.py:88
  319.3 50.1 %all_to_all.57 = bf16[1,8,64,1024]{3,2,0,1:T(8,128)(2,1)S(1)} all-to-all(bf16[1,8,64,1024]{3,2,0,1:T(8,128)(2,1)S(1)} %copy.194), channel_id=1, replica_groups=mesh['dp'=4,'seq'=4,'chan'=2] {'seq'}, dimensions={1} | all-to-all | bytes 2097152 | tf_op jit(solution)/shard_map/all_to_all | solution.py:93
  371.8 78.7 %all-reduce.10.cloned.1.call-done = (f32[2,512,512]{2,1,0:T(8,128)}, f32[2,512,512]{2,1,0:T(8,128)}) async-done(((f32[2,512,512]{2,1,0:T(8,128)}, f32[2,512,512]{2,1,0:T(8,128)}), (f32[2,512,512]{2,1,0:T(8,128)}, f32[2,512,512]{2,1,0:T(8,128)})) %all-reduce.10.cloned.1.call-update) | async-done | bytes 4194320 | tf_op jit(solution)/shard_map/psum | solution.py:101
  454.8 4.6 fusion.39
  462.9 43.2 %all-reduce = (f32[4,2,512]{0,1,2:T(2,128)S(1)}, f32[4,2,512]{0,1,2:T(2,128)}) all-reduce(f32[4,2,512]{0,1,2:T(2,128)S(1)} %fusion.39, f32[4,2,512]{0,1,2:T(2,128)} %fusion.42), channel_id=1, replica_groups=mesh['dp'=4,'seq'=4,'chan'=2] {'seq'}, use_global_device_ids=true, to_apply=%region_6.0 | all-reduce | flops 8192 | bytes 65536 | tf_op jit(solution)/shard_map/psum | solution.py:101
  506.1 26.7 %all-reduce.2 = (f32[4,2,512]{0,1,2:T(2,128)S(1)}, f32[4,2,512]{0,1,2:T(2,128)}) all-reduce(f32[4,2,512]{0,1,2:T(2,128)S(1)} %get-tuple-element.42, f32[4,2,512]{0,1,2:T(2,128)} %get-tuple-element.43), channel_id=1, replica_groups=mesh['dp'=4,'seq'=4,'chan'=2] {'dp'}, use_global_device_ids=true, to_apply=%region_7.0 | all-reduce | flops 8192 | bytes 65536 | tf_op jit(solution)/shard_map/psum | solution.py:100
  541.1 39.9 %psum.71 = f32[8,8]{1,0:T(8,128)S(1)} all-reduce(f32[8,8]{1,0:T(8,128)S(1)} %convolution_bitcast_fusion.3), channel_id=1, replica_groups=mesh['dp'=4,'seq'=4,'chan'=2] {'dp','seq','chan'}, use_global_device_ids=true, to_apply=%region_1.0 | all-reduce | flops 64 | bytes 512 | tf_op jit(solution)/shard_map/psum | solution.py:99
  586.4 85.6 %all-reduce.12.cloned.1.call-done = (f32[2,512,512]{2,1,0:T(8,128)}, f32[2,512,512]{2,1,0:T(8,128)}) async-done(((f32[2,512,512]{2,1,0:T(8,128)}, f32[2,512,512]{2,1,0:T(8,128)}), (f32[2,512,512]{2,1,0:T(8,128)}, f32[2,512,512]{2,1,0:T(8,128)})) %all-reduce.12.cloned.1.call-update) | async-done | bytes 4194320 | tf_op jit(solution)/shard_map/psum | solution.py:100
  672.0 4.7 broadcast_multiply_fusion
  (110 shorter events, 78.7 us)
Async XLA Ops:
  7.2 73.3 %copy-start = (bf16[2,512,512]{2,1,0:T(8,128)(2,1)S(1)}, bf16[2,512,512]{2,1,0:T(8,128)(2,1)}, u32[]{:S(2)}) copy-start(bf16[2,512,512]{2,1,0:T(8,128)(2,1)} %param.12) | copy-start | bytes 3145732
  7.2 105.6 %all-gather.5.cloned.1.call-start = ((), (), s32[]{:S(2)}) async-start(), calls=%async_computation.4 | async-start | bytes 3145728 | tf_op jit(solution)/shard_map/all_gather | solution.py:50
  42.3 1.6 copy-start.19
  72.9 1.2 copy-start.9
  74.5 4.0 copy-start.13
  80.3 2.1 copy-start.17
  80.4 3.0 copy-start.18
  80.4 67.6 %all-gather.7.cloned.1.call-start = ((), (), s32[]{:S(2)}) async-start(), calls=%async_computation.5 | async-start | bytes 3145728 | tf_op jit(solution)/shard_map/all_gather | solution.py:45
  82.2 117.9 %all-gather.11.cloned.1.call-start = ((), (), s32[]{:S(2)}) async-start(), calls=%async_computation.7 | async-start | bytes 3145728 | tf_op jit(solution)/shard_map/all_gather | solution.py:58
  166.8 68.4 %all-gather.9.cloned.1.call-start = ((), (), s32[]{:S(2)}) async-start(), calls=%async_computation.6 | async-start | bytes 3145728 | tf_op jit(solution)/shard_map/all_gather | solution.py:57
  169.2 281.3 %all-reduce.10.cloned.1.call-start = ((), (), s32[]{:S(2)}) async-start(), calls=%async_computation.9 | async-start | bytes 8388608 | tf_op jit(solution)/shard_map/psum | solution.py:101
  250.6 1.2 copy-start.11
  250.6 334.1 %all-reduce.8.cloned.1.call-start = ((), (), s32[]{:S(2)}) async-start(), calls=%async_computation.8 | async-start | bytes 524288 | tf_op jit(solution)/shard_map/psum | solution.py:99
  251.8 1.6 copy-start.12
  251.8 1.9 copy-start.14
  257.1 59.2 %copy-start.5 = (bf16[1,2,256,2,512]{2,4,3,1,0:T(8,128)(2,1)}, bf16[1,2,256,2,512]{2,4,3,1,0:T(8,128)(2,1)S(1)}, u32[]{:S(2)}) copy-start(bf16[1,2,256,2,512]{2,4,3,1,0:T(8,128)(2,1)S(1)} %copy.189) | copy-start | bytes 3145732
  319.3 51.2 %copy-start.10 = (bf16[1,2,256,1024]{3,2,1,0:T(8,128)(2,1)S(1)}, bf16[1,2,256,1024]{3,2,1,0:T(8,128)(2,1)}, u32[]{:S(2)}) copy-start(bf16[1,2,256,1024]{3,2,1,0:T(8,128)(2,1)} %param.8) | copy-start | bytes 3145732
  371.7 300.3 %all-reduce.12.cloned.1.call-start = ((), (), s32[]{:S(2)}) async-start(), calls=%async_computation.10 | async-start | bytes 8388608 | tf_op jit(solution)/shard_map/psum | solution.py:100
  450.5 1.2 copy-start.4
  450.5 3.3 copy-start.3
  454.8 4.6 copy-start.15
  506.0 33.0 %copy-start.2 = (bf16[8,64,1024]{2,0,1:T(8,128)(2,1)S(1)}, bf16[8,64,1024]{2,0,1:T(8,128)(2,1)}, u32[]{:S(2)}) copy-start(bf16[8,64,1024]{2,0,1:T(8,128)(2,1)} %copy-done.1) | copy-start | bytes 3145732
  535.3 46.3 %copy-start.6 = (bf16[1,2,256,2,512]{2,4,3,1,0:T(8,128)(2,1)S(1)}, bf16[1,2,256,2,512]{2,4,3,1,0:T(8,128)(2,1)}, u32[]{:S(2)}) copy-start(bf16[1,2,256,2,512]{2,4,3,1,0:T(8,128)(2,1)} %copy-done.5) | copy-start | bytes 3145732
  535.3 46.3 %copy-start.16 = (bf16[256,256]{1,0:T(8,128)(2,1)S(1)}, bf16[256,256]{1,0:T(8,128)(2,1)}, u32[]{:S(2)}) copy-start(bf16[256,256]{1,0:T(8,128)(2,1)} %param.10) | copy-start | bytes 393220
  (3 other events, 3.1 us)
Sparse Core Ops, SparseCore 0:
  80.5 32.2 all-gather.4
  114.8 33.1 all-gather.6
  166.9 33.1 all-gather.10
  202.1 33.1 all-gather.8
  250.7 199.7 all-reduce.9
  457.3 127.3 all-reduce.7
  587.3 84.6 all-reduce.11
